TPU v7x, 512 devices: a whole 4x4x16 slice. The times are simulated.
512 devices in a mesh: dp: 8 (over y, core), ctx: 64 (over z, x).
Axes of the slice: x: 4, y: 4, z: 16, core: 2. Of those that a mesh axis runs over, the one named last changes fastest.
Arguments:
- query_in: bfloat16 [8, 8192, 1792], P('dp', 'ctx'), may hold values from -8 to 8
- key_in: bfloat16 [8, 8192, 256], P('dp', 'ctx'), may hold values from -4 to 4
- value_input: bfloat16 [8, 8192, 256], P('dp', 'ctx'), may hold values from -4 to 4
- output_gradient: bfloat16 [8, 8192, 1792], P('dp', 'ctx'), may hold values from -5 to 5
- doc_ids: int32 [8, 8192], P('dp', 'ctx'), may hold values from 0 to 1, as said below
- query_bias: float32 [1792], replicated, may hold values from -2 to 2
Outputs:
- attended: bfloat16 [8, 8192, 1792], P('dp', 'ctx')
- grad_query: bfloat16 [8, 8192, 1792], P('dp', 'ctx')
- key_gradient: bfloat16 [8, 8192, 256], P('dp', 'ctx')
- value_gradient: bfloat16 [8, 8192, 256], P('dp', 'ctx')
- grad_bias: float32 [1792], replicated
Inputs may be any that keep to these rules, and one draw needn't show every extreme that they name: `doc_ids`: ids never fall along a sequence; each of the 2 documents of a sequence holds 2048 to 6144 tokens, and together they fill all 8192 tokens.
All inputs are finite; a program needn't handle non-finite values.
Results may differ from a plain program's by a relative error of at most 0.019.
Values may be sent and summed in bfloat16 or wider, within the bound.
A program may use at most 64 MiB of HBM per device.

v0:
```python
import math

import jax
import jax.numpy as jnp
from jax import lax
from jax.sharding import PartitionSpec as P

QUERY_HEADS = 14
KEY_VALUE_HEADS = 2
HEAD_SIZE = 128
GROUP_SIZE = 7
BLK = 128
WB = 16


def passed_along(value, axis, steps):
    count = lax.axis_size(axis)
    first, last = (max(0, -steps), min(count, count - steps))
    return lax.ppermute(value, axis, [(source, source + steps) for source in range(first, last)])


def split_pack(packed_block):
    head_size_width = KEY_VALUE_HEADS * HEAD_SIZE
    key_head_rows = packed_block[:, :head_size_width].reshape(
        packed_block.shape[0], KEY_VALUE_HEADS, HEAD_SIZE
    )
    value_head_rows = packed_block[:, head_size_width:].reshape(
        packed_block.shape[0], KEY_VALUE_HEADS, HEAD_SIZE
    )
    return (key_head_rows, value_head_rows)


def local(query_in, key_in, value_input, output_gradient, doc_ids, query_bias):
    sharded_rows = query_in.shape[1]
    ctx_count = lax.axis_size("ctx")
    ctx_rank = lax.axis_index("ctx")
    score_scale = 1.0 / math.sqrt(HEAD_SIZE)
    blocks_here = sharded_rows // BLK
    window_slots = min((WB - 1 + blocks_here - 1) // blocks_here, ctx_count - 1) + 1
    group_slots = max(1, min(window_slots, 512 // sharded_rows))
    group_count = -(-window_slots // group_slots)
    padded_slots = group_count * group_slots
    grouped_rows = group_slots * sharded_rows
    packed_width = 2 * KEY_VALUE_HEADS * HEAD_SIZE
    query_rows = (query_in[0].astype(jnp.float32) + query_bias).astype(jnp.bfloat16)
    query_head_rows = query_rows.reshape(sharded_rows, KEY_VALUE_HEADS, GROUP_SIZE, HEAD_SIZE)
    gradient_heads = output_gradient[0].reshape(
        sharded_rows, KEY_VALUE_HEADS, GROUP_SIZE, HEAD_SIZE
    )
    own_pack = jnp.concatenate([key_in[0], value_input[0]], axis=1)
    own_docs = doc_ids[0]
    query_pos = ctx_rank * sharded_rows + jnp.arange(sharded_rows, dtype=jnp.int32)
    first_pack = jnp.concatenate(
        [own_pack[None], jnp.zeros((window_slots - 1, sharded_rows, packed_width), jnp.bfloat16)],
        axis=0,
    )
    first_docs = jnp.concatenate(
        [own_docs[None], jnp.zeros((window_slots - 1, sharded_rows), jnp.int32)], axis=0
    )

    def pass_on(step_index, running):
        stored_pack, stored_docs, moving_pack, moving_docs = running
        moving_pack, moving_docs = passed_along((moving_pack, moving_docs), "ctx", 1)
        stored_pack = lax.dynamic_update_index_in_dim(stored_pack, moving_pack, step_index, 0)
        stored_docs = lax.dynamic_update_index_in_dim(stored_docs, moving_docs, step_index, 0)
        return (stored_pack, stored_docs, moving_pack, moving_docs)

    window_pack, window_docs, _, _ = lax.fori_loop(
        1, window_slots, pass_on, (first_pack, first_docs, own_pack, own_docs)
    )
    spare_slots = padded_slots - window_slots
    window_pack = jnp.concatenate(
        [window_pack, jnp.zeros((spare_slots, sharded_rows, packed_width), jnp.bfloat16)], axis=0
    )
    window_pack = window_pack.reshape(group_count, grouped_rows, packed_width)
    window_docs = jnp.concatenate(
        [window_docs, jnp.zeros((spare_slots, sharded_rows), jnp.int32)], axis=0
    )
    window_docs = window_docs.reshape(group_count, grouped_rows)
    group_ids = jnp.arange(group_count, dtype=jnp.int32)

    def group_mask(group_index, docs_block):
        key_index = jnp.arange(grouped_rows, dtype=jnp.int32)
        slot_index = group_index * group_slots + key_index // sharded_rows
        key_pos = (ctx_rank - slot_index) * sharded_rows + key_index % sharded_rows
        inside = ((slot_index < window_slots) & (key_pos >= 0))[None, :]
        causal = key_pos[None, :] <= query_pos[:, None]
        near = query_pos[:, None] // BLK - key_pos[None, :] // BLK < WB
        same_doc = own_docs[:, None] == docs_block[None, :]
        return inside & causal & near & same_doc

    def group_scores(packed_block, allowed):
        key_head_rows, value_head_rows = split_pack(packed_block)
        scores = (
            jnp.einsum(
                "qgnd,kgd->gnqk", query_head_rows, key_head_rows, preferred_element_type=jnp.float32
            )
            * score_scale
        )
        return (jnp.where(allowed[None, None], scores, -jnp.inf), key_head_rows, value_head_rows)

    def forward_work(running, packed_block, allowed):
        row_max, row_sum, weighted = running
        scores, key_head_rows, value_head_rows = group_scores(packed_block, allowed)
        new_max = jnp.maximum(row_max, jnp.max(scores, axis=-1))
        rescale = jnp.exp(row_max - new_max)
        weights = jnp.exp(scores - new_max[..., None])
        row_sum = row_sum * rescale + jnp.sum(weights, axis=-1)
        weighted = weighted * rescale[..., None] + jnp.einsum(
            "gnqk,kgd->gnqd", weights, value_head_rows.astype(jnp.float32)
        )
        return (new_max, row_sum, weighted)

    def forward_step(running, inputs):
        packed_block, docs_block, group_index = inputs
        allowed = group_mask(group_index, docs_block)
        running = forward_work(running, packed_block, allowed)
        return (running, None)

    statistics_shape = (KEY_VALUE_HEADS, GROUP_SIZE, sharded_rows)
    start_stats = (
        jnp.full(statistics_shape, -jnp.inf, jnp.float32),
        jnp.zeros(statistics_shape, jnp.float32),
        jnp.zeros(statistics_shape + (HEAD_SIZE,), jnp.float32),
    )
    (row_max, row_sum, weighted), _ = lax.scan(
        forward_step, start_stats, (window_pack, window_docs, group_ids)
    )
    log_total = row_max + jnp.log(row_sum)
    attended = jnp.transpose(weighted / row_sum[..., None], (2, 0, 1, 3)).astype(jnp.bfloat16)
    row_dot = jnp.einsum(
        "qgnd,qgnd->gnq", gradient_heads, attended, preferred_element_type=jnp.float32
    )

    def backward_work(grad_query, packed_block, allowed):
        scores, key_head_rows, value_head_rows = group_scores(packed_block, allowed)
        attend = jnp.exp(scores - log_total[..., None])
        grad_prob = jnp.einsum(
            "qgnd,kgd->gnqk", gradient_heads, value_head_rows, preferred_element_type=jnp.float32
        )
        grad_score = (attend * (grad_prob - row_dot[..., None])).astype(jnp.bfloat16)
        grad_query = grad_query + jnp.einsum(
            "gnqk,kgd->qgnd", grad_score, key_head_rows, preferred_element_type=jnp.float32
        )
        key_gradient = (
            jnp.einsum(
                "gnqk,qgnd->kgd", grad_score, query_head_rows, preferred_element_type=jnp.float32
            )
            * score_scale
        )
        value_gradient = jnp.einsum(
            "gnqk,qgnd->kgd",
            attend.astype(jnp.bfloat16),
            gradient_heads,
            preferred_element_type=jnp.float32,
        )
        partial_value = jnp.concatenate(
            [
                key_gradient.reshape(grouped_rows, KEY_VALUE_HEADS * HEAD_SIZE),
                value_gradient.reshape(grouped_rows, KEY_VALUE_HEADS * HEAD_SIZE),
            ],
            axis=1,
        )
        return (grad_query, partial_value)

    def backward_step(grad_query, inputs):
        packed_block, docs_block, group_index = inputs
        allowed = group_mask(group_index, docs_block)
        return backward_work(grad_query, packed_block, allowed)

    grad_query, partials = lax.scan(
        backward_step,
        jnp.zeros((sharded_rows, KEY_VALUE_HEADS, GROUP_SIZE, HEAD_SIZE), jnp.float32),
        (window_pack, window_docs, group_ids),
    )
    partials = partials.reshape(padded_slots, sharded_rows, packed_width)
    query_grad = (grad_query * score_scale).reshape(sharded_rows, QUERY_HEADS * HEAD_SIZE)

    def return_partial(step_index, running):
        returned = passed_along(running, "ctx", -1)
        return returned + lax.dynamic_index_in_dim(
            partials, window_slots - 1 - step_index, 0, keepdims=False
        )

    summed_total = lax.fori_loop(1, window_slots, return_partial, partials[window_slots - 1])
    key_gradient = summed_total[:, : KEY_VALUE_HEADS * HEAD_SIZE].astype(jnp.bfloat16)
    value_gradient = summed_total[:, KEY_VALUE_HEADS * HEAD_SIZE :].astype(jnp.bfloat16)
    grad_bias = lax.psum(jnp.sum(query_grad, axis=0), ("dp", "ctx"))
    attended_out = attended.reshape(sharded_rows, QUERY_HEADS * HEAD_SIZE)
    return (
        attended_out[None],
        query_grad.astype(jnp.bfloat16)[None],
        key_gradient[None],
        value_gradient[None],
        grad_bias,
    )


def solution(mesh):
    placed = (
        P("dp", "ctx", None),
        P("dp", "ctx", None),
        P("dp", "ctx", None),
        P("dp", "ctx", None),
        P("dp", "ctx"),
        P(),
    )
    return jax.shard_map(
        local,
        mesh=mesh,
        in_specs=placed,
        out_specs=(
            P("dp", "ctx", None),
            P("dp", "ctx", None),
            P("dp", "ctx", None),
            P("dp", "ctx", None),
            P(),
        ),
        check_vma=False,
    )
```

profile of v0, /device:TPU:1, one launch (start us, length us, event | category | flops | bytes accessed | tf_op | source)
XLA Modules:
  0.0 563.7 jit_solution(16847469983181574787)
XLA Ops:
  8.9 138.4 %while.72 = (s32[]{:T(128)}, bf16[16,128,512]{2,1,0:T(8,128)(2,1)}, s32[16,128]{1,0:T(8,128)S(1)}, bf16[128,512]{1,0:T(8,128)(2,1)S(1)}, s32[128]{0:T(128)S(1)}, /*index=5*/s32[]{:T(128)}, s32[]{:T(128)}, s32[]{:T(128)}) while((s32[]{:T(128)}, bf16[16,128,512]{2,1,0:T(8,128)(2,1)}, s32[16,128]{1,0:T(8,128)S(1)}, ...), condition=%wide.region_1.2_spmd, body=%wide.region_0.1_spmd.sunk | while | flops 5 | bytes 1052879 | solution.py:68
  29.2 4.8 collective-permute-start.1
  102.5 4.8 collective-permute-start.1
  131.0 4.5 collective-permute-start.1
  140.5 5.3 collective-permute-start.1
  151.5 23.1 %while.74 = (s32[]{:T(128)}, f32[2,7,128]{2,1,0:T(8,128)S(1)}, f32[2,7,128]{2,1,0:T(8,128)S(1)}, f32[2,7,128,128]{3,2,1,0:T(8,128)S(1)}, s32[4]{0:T(128)S(1)}, /...) while((s32[]{:T(128)}, f32[2,7,128]{2,1,0:T(8,128)S(1)}, ...), condition=%wide.region_5.6_spmd.clone.clone.clone, body=%wide.region_2.5_spmd.clone.clone.clone.sunk | while | flops 480120704 | bytes 16320205 | solution.py:126
  179.3 42.8 %while.75 = (s32[]{:T(128)}, f32[128,2,7,128]{0,3,2,1:T(8,128)S(1)}, f32[4,512,512]{2,1,0:T(8,128)}, bf16[4,512,512]{1,2,0:T(8,128)(2,1)}, s32[4]{0:T(128)S(1)},...) while((s32[]{:T(128)}, ...), condition=%wide.region_7.8_spmd.clone.clone.clone, body=%wide.region_6.7_spmd.clone.clone.clone.sunk | while | flops 1184918656 | bytes 30644960 | solution.py:171
  223.1 163.2 %while.73 = (s32[]{:T(128)}, f32[128,512]{1,0:T(8,128)S(1)}, f32[16,128,512]{2,1,0:T(8,128)}, s32[]{:T(128)}, s32[]{:T(128)}, /*index=5*/s32[]{:T(128)}, s32[]{:T(128)}) while((s32[]{:T(128)}, f32[128,512]{1,0:T(8,128)S(1)}, f32[16,128,512]{2,1,0:T(8,128)}, s32[]{:T(128)}, s32[]{:T(128)}, /*index=5*/s32[]{:T(128)}, s32[]{:T(128)}) %tuple.177), condition=%wide.region_9.10_spmd, body=%wide.region_8.9_spmd.sunk | while | flops 65542 | bytes 1835175 | solution.py:185
  224.4 6.0 %collective-permute-done.2 = f32[128,512]{1,0:T(8,128)S(1)} collective-permute-done((f32[128,512]{1,0:T(8,128)S(1)}, f32[128,512]{1,0:T(8,128)S(1)}, u32[]{:S(2)}, u32[]{:S(2)}) %collective-permute-start.2) | collective-permute-done | bytes 262176 | tf_op jit(solution)/shard_map/while/body/eval_jaxpr/ppermute | solution.py:19
  232.7 7.8 %collective-permute-done.2 = f32[128,512]{1,0:T(8,128)S(1)} collective-permute-done((f32[128,512]{1,0:T(8,128)S(1)}, f32[128,512]{1,0:T(8,128)S(1)}, u32[]{:S(2)}, u32[]{:S(2)}) %collective-permute-start.2) | collective-permute-done | bytes 262176 | tf_op jit(solution)/shard_map/while/body/eval_jaxpr/ppermute | solution.py:19
  242.8 7.7 %collective-permute-done.2 = f32[128,512]{1,0:T(8,128)S(1)} collective-permute-done((f32[128,512]{1,0:T(8,128)S(1)}, f32[128,512]{1,0:T(8,128)S(1)}, u32[]{:S(2)}, u32[]{:S(2)}) %collective-permute-start.2) | collective-permute-done | bytes 262176 | tf_op jit(solution)/shard_map/while/body/eval_jaxpr/ppermute | solution.py:19
  252.8 10.2 %collective-permute-done.2 = f32[128,512]{1,0:T(8,128)S(1)} collective-permute-done((f32[128,512]{1,0:T(8,128)S(1)}, f32[128,512]{1,0:T(8,128)S(1)}, u32[]{:S(2)}, u32[]{:S(2)}) %collective-permute-start.2) | collective-permute-done | bytes 262176 | tf_op jit(solution)/shard_map/while/body/eval_jaxpr/ppermute | solution.py:19
  265.3 11.4 %collective-permute-done.2 = f32[128,512]{1,0:T(8,128)S(1)} collective-permute-done((f32[128,512]{1,0:T(8,128)S(1)}, f32[128,512]{1,0:T(8,128)S(1)}, u32[]{:S(2)}, u32[]{:S(2)}) %collective-permute-start.2) | collective-permute-done | bytes 262176 | tf_op jit(solution)/shard_map/while/body/eval_jaxpr/ppermute | solution.py:19
  279.0 9.2 %collective-permute-done.2 = f32[128,512]{1,0:T(8,128)S(1)} collective-permute-done((f32[128,512]{1,0:T(8,128)S(1)}, f32[128,512]{1,0:T(8,128)S(1)}, u32[]{:S(2)}, u32[]{:S(2)}) %collective-permute-start.2) | collective-permute-done | bytes 262176 | tf_op jit(solution)/shard_map/while/body/eval_jaxpr/ppermute | solution.py:19
  290.5 7.4 %collective-permute-done.2 = f32[128,512]{1,0:T(8,128)S(1)} collective-permute-done((f32[128,512]{1,0:T(8,128)S(1)}, f32[128,512]{1,0:T(8,128)S(1)}, u32[]{:S(2)}, u32[]{:S(2)}) %collective-permute-start.2) | collective-permute-done | bytes 262176 | tf_op jit(solution)/shard_map/while/body/eval_jaxpr/ppermute | solution.py:19
  300.1 6.8 %collective-permute-done.2 = f32[128,512]{1,0:T(8,128)S(1)} collective-permute-done((f32[128,512]{1,0:T(8,128)S(1)}, f32[128,512]{1,0:T(8,128)S(1)}, u32[]{:S(2)}, u32[]{:S(2)}) %collective-permute-start.2) | collective-permute-done | bytes 262176 | tf_op jit(solution)/shard_map/while/body/eval_jaxpr/ppermute | solution.py:19
  309.3 7.6 %collective-permute-done.2 = f32[128,512]{1,0:T(8,128)S(1)} collective-permute-done((f32[128,512]{1,0:T(8,128)S(1)}, f32[128,512]{1,0:T(8,128)S(1)}, u32[]{:S(2)}, u32[]{:S(2)}) %collective-permute-start.2) | collective-permute-done | bytes 262176 | tf_op jit(solution)/shard_map/while/body/eval_jaxpr/ppermute | solution.py:19
  319.2 7.9 %collective-permute-done.2 = f32[128,512]{1,0:T(8,128)S(1)} collective-permute-done((f32[128,512]{1,0:T(8,128)S(1)}, f32[128,512]{1,0:T(8,128)S(1)}, u32[]{:S(2)}, u32[]{:S(2)}) %collective-permute-start.2) | collective-permute-done | bytes 262176 | tf_op jit(solution)/shard_map/while/body/eval_jaxpr/ppermute | solution.py:19
  329.4 7.9 %collective-permute-done.2 = f32[128,512]{1,0:T(8,128)S(1)} collective-permute-done((f32[128,512]{1,0:T(8,128)S(1)}, f32[128,512]{1,0:T(8,128)S(1)}, u32[]{:S(2)}, u32[]{:S(2)}) %collective-permute-start.2) | collective-permute-done | bytes 262176 | tf_op jit(solution)/shard_map/while/body/eval_jaxpr/ppermute | solution.py:19
  339.7 7.9 %collective-permute-done.2 = f32[128,512]{1,0:T(8,128)S(1)} collective-permute-done((f32[128,512]{1,0:T(8,128)S(1)}, f32[128,512]{1,0:T(8,128)S(1)}, u32[]{:S(2)}, u32[]{:S(2)}) %collective-permute-start.2) | collective-permute-done | bytes 262176 | tf_op jit(solution)/shard_map/while/body/eval_jaxpr/ppermute | solution.py:19
  349.9 8.8 %collective-permute-done.2 = f32[128,512]{1,0:T(8,128)S(1)} collective-permute-done((f32[128,512]{1,0:T(8,128)S(1)}, f32[128,512]{1,0:T(8,128)S(1)}, u32[]{:S(2)}, u32[]{:S(2)}) %collective-permute-start.2) | collective-permute-done | bytes 262176 | tf_op jit(solution)/shard_map/while/body/eval_jaxpr/ppermute | solution.py:19
  361.0 10.4 %collective-permute-done.2 = f32[128,512]{1,0:T(8,128)S(1)} collective-permute-done((f32[128,512]{1,0:T(8,128)S(1)}, f32[128,512]{1,0:T(8,128)S(1)}, u32[]{:S(2)}, u32[]{:S(2)}) %collective-permute-start.2) | collective-permute-done | bytes 262176 | tf_op jit(solution)/shard_map/while/body/eval_jaxpr/ppermute | solution.py:19
  373.7 11.5 %collective-permute-done.2 = f32[128,512]{1,0:T(8,128)S(1)} collective-permute-done((f32[128,512]{1,0:T(8,128)S(1)}, f32[128,512]{1,0:T(8,128)S(1)}, u32[]{:S(2)}, u32[]{:S(2)}) %collective-permute-start.2) | collective-permute-done | bytes 262176 | tf_op jit(solution)/shard_map/while/body/eval_jaxpr/ppermute | solution.py:19
  387.3 175.4 %psum.7 = f32[1792]{0:T(1024)} all-reduce(f32[1792]{0:T(1024)S(1)} %reduce_sum.25), channel_id=1, replica_groups=mesh['dp'=8,'ctx'=64] {'dp','ctx'}, use_global_device_ids=true, to_apply=%region_11.12 | all-reduce | flops 1792 | bytes 14336 | tf_op jit(solution)/shard_map/psum | solution.py:188
  (298 shorter events, 232.6 us)
Async XLA Ops:
  25.7 9.1 %collective-permute-start = (bf16[128,512]{1,0:T(8,128)(2,1)S(1)}, bf16[128,512]{1,0:T(8,128)(2,1)S(1)}, u32[]{:S(2)}, u32[]{:S(2)}) collective-permute-start(bf16[128,512]{1,0:T(8,128)(2,1)S(1)} %get-tuple-element.1222), channel_id=1, source_target_pairs={{0,1},{1,2},{2,3},{3,4},{4,5},{5,6},{6,7},{7,8},{8,9},{9,10},{10,1... | collective-permute-start | bytes 393224 | tf_op jit(solution)/shard_map/while/body/eval_jaxpr/ppermute | solution.py:19
  35.5 8.3 %collective-permute-start = (bf16[128,512]{1,0:T(8,128)(2,1)S(1)}, bf16[128,512]{1,0:T(8,128)(2,1)S(1)}, u32[]{:S(2)}, u32[]{:S(2)}) collective-permute-start(bf16[128,512]{1,0:T(8,128)(2,1)S(1)} %get-tuple-element.1222), channel_id=1, source_target_pairs={{0,1},{1,2},{2,3},{3,4},{4,5},{5,6},{6,7},{7,8},{8,9},{9,10},{10,1... | collective-permute-start | bytes 393224 | tf_op jit(solution)/shard_map/while/body/eval_jaxpr/ppermute | solution.py:19
  44.5 8.3 %collective-permute-start = (bf16[128,512]{1,0:T(8,128)(2,1)S(1)}, bf16[128,512]{1,0:T(8,128)(2,1)S(1)}, u32[]{:S(2)}, u32[]{:S(2)}) collective-permute-start(bf16[128,512]{1,0:T(8,128)(2,1)S(1)} %get-tuple-element.1222), channel_id=1, source_target_pairs={{0,1},{1,2},{2,3},{3,4},{4,5},{5,6},{6,7},{7,8},{8,9},{9,10},{10,1... | collective-permute-start | bytes 393224 | tf_op jit(solution)/shard_map/while/body/eval_jaxpr/ppermute | solution.py:19
  53.5 8.3 %collective-permute-start = (bf16[128,512]{1,0:T(8,128)(2,1)S(1)}, bf16[128,512]{1,0:T(8,128)(2,1)S(1)}, u32[]{:S(2)}, u32[]{:S(2)}) collective-permute-start(bf16[128,512]{1,0:T(8,128)(2,1)S(1)} %get-tuple-element.1222), channel_id=1, source_target_pairs={{0,1},{1,2},{2,3},{3,4},{4,5},{5,6},{6,7},{7,8},{8,9},{9,10},{10,1... | collective-permute-start | bytes 393224 | tf_op jit(solution)/shard_map/while/body/eval_jaxpr/ppermute | solution.py:19
  62.6 8.3 %collective-permute-start = (bf16[128,512]{1,0:T(8,128)(2,1)S(1)}, bf16[128,512]{1,0:T(8,128)(2,1)S(1)}, u32[]{:S(2)}, u32[]{:S(2)}) collective-permute-start(bf16[128,512]{1,0:T(8,128)(2,1)S(1)} %get-tuple-element.1222), channel_id=1, source_target_pairs={{0,1},{1,2},{2,3},{3,4},{4,5},{5,6},{6,7},{7,8},{8,9},{9,10},{10,1... | collective-permute-start | bytes 393224 | tf_op jit(solution)/shard_map/while/body/eval_jaxpr/ppermute | solution.py:19
  80.6 8.4 %collective-permute-start = (bf16[128,512]{1,0:T(8,128)(2,1)S(1)}, bf16[128,512]{1,0:T(8,128)(2,1)S(1)}, u32[]{:S(2)}, u32[]{:S(2)}) collective-permute-start(bf16[128,512]{1,0:T(8,128)(2,1)S(1)} %get-tuple-element.1222), channel_id=1, source_target_pairs={{0,1},{1,2},{2,3},{3,4},{4,5},{5,6},{6,7},{7,8},{8,9},{9,10},{10,1... | collective-permute-start | bytes 393224 | tf_op jit(solution)/shard_map/while/body/eval_jaxpr/ppermute | solution.py:19
  89.7 8.6 %collective-permute-start = (bf16[128,512]{1,0:T(8,128)(2,1)S(1)}, bf16[128,512]{1,0:T(8,128)(2,1)S(1)}, u32[]{:S(2)}, u32[]{:S(2)}) collective-permute-start(bf16[128,512]{1,0:T(8,128)(2,1)S(1)} %get-tuple-element.1222), channel_id=1, source_target_pairs={{0,1},{1,2},{2,3},{3,4},{4,5},{5,6},{6,7},{7,8},{8,9},{9,10},{10,1... | collective-permute-start | bytes 393224 | tf_op jit(solution)/shard_map/while/body/eval_jaxpr/ppermute | solution.py:19
  99.0 9.1 %collective-permute-start = (bf16[128,512]{1,0:T(8,128)(2,1)S(1)}, bf16[128,512]{1,0:T(8,128)(2,1)S(1)}, u32[]{:S(2)}, u32[]{:S(2)}) collective-permute-start(bf16[128,512]{1,0:T(8,128)(2,1)S(1)} %get-tuple-element.1222), channel_id=1, source_target_pairs={{0,1},{1,2},{2,3},{3,4},{4,5},{5,6},{6,7},{7,8},{8,9},{9,10},{10,1... | collective-permute-start | bytes 393224 | tf_op jit(solution)/shard_map/while/body/eval_jaxpr/ppermute | solution.py:19
  108.8 8.6 %collective-permute-start = (bf16[128,512]{1,0:T(8,128)(2,1)S(1)}, bf16[128,512]{1,0:T(8,128)(2,1)S(1)}, u32[]{:S(2)}, u32[]{:S(2)}) collective-permute-start(bf16[128,512]{1,0:T(8,128)(2,1)S(1)} %get-tuple-element.1222), channel_id=1, source_target_pairs={{0,1},{1,2},{2,3},{3,4},{4,5},{5,6},{6,7},{7,8},{8,9},{9,10},{10,1... | collective-permute-start | bytes 393224 | tf_op jit(solution)/shard_map/while/body/eval_jaxpr/ppermute | solution.py:19
  127.1 9.1 %collective-permute-start = (bf16[128,512]{1,0:T(8,128)(2,1)S(1)}, bf16[128,512]{1,0:T(8,128)(2,1)S(1)}, u32[]{:S(2)}, u32[]{:S(2)}) collective-permute-start(bf16[128,512]{1,0:T(8,128)(2,1)S(1)} %get-tuple-element.1222), channel_id=1, source_target_pairs={{0,1},{1,2},{2,3},{3,4},{4,5},{5,6},{6,7},{7,8},{8,9},{9,10},{10,1... | collective-permute-start | bytes 393224 | tf_op jit(solution)/shard_map/while/body/eval_jaxpr/ppermute | solution.py:19
  137.0 9.7 %collective-permute-start = (bf16[128,512]{1,0:T(8,128)(2,1)S(1)}, bf16[128,512]{1,0:T(8,128)(2,1)S(1)}, u32[]{:S(2)}, u32[]{:S(2)}) collective-permute-start(bf16[128,512]{1,0:T(8,128)(2,1)S(1)} %get-tuple-element.1222), channel_id=1, source_target_pairs={{0,1},{1,2},{2,3},{3,4},{4,5},{5,6},{6,7},{7,8},{8,9},{9,10},{10,1... | collective-permute-start | bytes 393224 | tf_op jit(solution)/shard_map/while/body/eval_jaxpr/ppermute | solution.py:19
  231.4 9.1 %collective-permute-start.2 = (f32[128,512]{1,0:T(8,128)S(1)}, f32[128,512]{1,0:T(8,128)S(1)}, u32[]{:S(2)}, u32[]{:S(2)}) collective-permute-start(f32[128,512]{1,0:T(8,128)S(1)} %get-tuple-element.1333), channel_id=1, source_target_pairs={{1,0},{2,1},{3,2},{4,3},{5,4},{6,5},{7,6},{8,7},{9,8},{10,9},{11,1... | collective-permute-start | bytes 786440 | tf_op jit(solution)/shard_map/while/body/eval_jaxpr/ppermute | solution.py:19
  241.5 9.0 %collective-permute-start.2 = (f32[128,512]{1,0:T(8,128)S(1)}, f32[128,512]{1,0:T(8,128)S(1)}, u32[]{:S(2)}, u32[]{:S(2)}) collective-permute-start(f32[128,512]{1,0:T(8,128)S(1)} %get-tuple-element.1333), channel_id=1, source_target_pairs={{1,0},{2,1},{3,2},{4,3},{5,4},{6,5},{7,6},{8,7},{9,8},{10,9},{11,1... | collective-permute-start | bytes 786440 | tf_op jit(solution)/shard_map/while/body/eval_jaxpr/ppermute | solution.py:19
  251.5 11.5 %collective-permute-start.2 = (f32[128,512]{1,0:T(8,128)S(1)}, f32[128,512]{1,0:T(8,128)S(1)}, u32[]{:S(2)}, u32[]{:S(2)}) collective-permute-start(f32[128,512]{1,0:T(8,128)S(1)} %get-tuple-element.1333), channel_id=1, source_target_pairs={{1,0},{2,1},{3,2},{4,3},{5,4},{6,5},{7,6},{8,7},{9,8},{10,9},{11,1... | collective-permute-start | bytes 786440 | tf_op jit(solution)/shard_map/while/body/eval_jaxpr/ppermute | solution.py:19
  264.0 12.7 %collective-permute-start.2 = (f32[128,512]{1,0:T(8,128)S(1)}, f32[128,512]{1,0:T(8,128)S(1)}, u32[]{:S(2)}, u32[]{:S(2)}) collective-permute-start(f32[128,512]{1,0:T(8,128)S(1)} %get-tuple-element.1333), channel_id=1, source_target_pairs={{1,0},{2,1},{3,2},{4,3},{5,4},{6,5},{7,6},{8,7},{9,8},{10,9},{11,1... | collective-permute-start | bytes 786440 | tf_op jit(solution)/shard_map/while/body/eval_jaxpr/ppermute | solution.py:19
  277.7 10.5 %collective-permute-start.2 = (f32[128,512]{1,0:T(8,128)S(1)}, f32[128,512]{1,0:T(8,128)S(1)}, u32[]{:S(2)}, u32[]{:S(2)}) collective-permute-start(f32[128,512]{1,0:T(8,128)S(1)} %get-tuple-element.1333), channel_id=1, source_target_pairs={{1,0},{2,1},{3,2},{4,3},{5,4},{6,5},{7,6},{8,7},{9,8},{10,9},{11,1... | collective-permute-start | bytes 786440 | tf_op jit(solution)/shard_map/while/body/eval_jaxpr/ppermute | solution.py:19
  289.2 8.7 %collective-permute-start.2 = (f32[128,512]{1,0:T(8,128)S(1)}, f32[128,512]{1,0:T(8,128)S(1)}, u32[]{:S(2)}, u32[]{:S(2)}) collective-permute-start(f32[128,512]{1,0:T(8,128)S(1)} %get-tuple-element.1333), channel_id=1, source_target_pairs={{1,0},{2,1},{3,2},{4,3},{5,4},{6,5},{7,6},{8,7},{9,8},{10,9},{11,1... | collective-permute-start | bytes 786440 | tf_op jit(solution)/shard_map/while/body/eval_jaxpr/ppermute | solution.py:19
  308.0 8.9 %collective-permute-start.2 = (f32[128,512]{1,0:T(8,128)S(1)}, f32[128,512]{1,0:T(8,128)S(1)}, u32[]{:S(2)}, u32[]{:S(2)}) collective-permute-start(f32[128,512]{1,0:T(8,128)S(1)} %get-tuple-element.1333), channel_id=1, source_target_pairs={{1,0},{2,1},{3,2},{4,3},{5,4},{6,5},{7,6},{8,7},{9,8},{10,9},{11,1... | collective-permute-start | bytes 786440 | tf_op jit(solution)/shard_map/while/body/eval_jaxpr/ppermute | solution.py:19
  317.9 9.2 %collective-permute-start.2 = (f32[128,512]{1,0:T(8,128)S(1)}, f32[128,512]{1,0:T(8,128)S(1)}, u32[]{:S(2)}, u32[]{:S(2)}) collective-permute-start(f32[128,512]{1,0:T(8,128)S(1)} %get-tuple-element.1333), channel_id=1, source_target_pairs={{1,0},{2,1},{3,2},{4,3},{5,4},{6,5},{7,6},{8,7},{9,8},{10,9},{11,1... | collective-permute-start | bytes 786440 | tf_op jit(solution)/shard_map/while/body/eval_jaxpr/ppermute | solution.py:19
  328.1 9.2 %collective-permute-start.2 = (f32[128,512]{1,0:T(8,128)S(1)}, f32[128,512]{1,0:T(8,128)S(1)}, u32[]{:S(2)}, u32[]{:S(2)}) collective-permute-start(f32[128,512]{1,0:T(8,128)S(1)} %get-tuple-element.1333), channel_id=1, source_target_pairs={{1,0},{2,1},{3,2},{4,3},{5,4},{6,5},{7,6},{8,7},{9,8},{10,9},{11,1... | collective-permute-start | bytes 786440 | tf_op jit(solution)/shard_map/while/body/eval_jaxpr/ppermute | solution.py:19
  338.4 9.2 %collective-permute-start.2 = (f32[128,512]{1,0:T(8,128)S(1)}, f32[128,512]{1,0:T(8,128)S(1)}, u32[]{:S(2)}, u32[]{:S(2)}) collective-permute-start(f32[128,512]{1,0:T(8,128)S(1)} %get-tuple-element.1333), channel_id=1, source_target_pairs={{1,0},{2,1},{3,2},{4,3},{5,4},{6,5},{7,6},{8,7},{9,8},{10,9},{11,1... | collective-permute-start | bytes 786440 | tf_op jit(solution)/shard_map/while/body/eval_jaxpr/ppermute | solution.py:19
  348.6 10.1 %collective-permute-start.2 = (f32[128,512]{1,0:T(8,128)S(1)}, f32[128,512]{1,0:T(8,128)S(1)}, u32[]{:S(2)}, u32[]{:S(2)}) collective-permute-start(f32[128,512]{1,0:T(8,128)S(1)} %get-tuple-element.1333), channel_id=1, source_target_pairs={{1,0},{2,1},{3,2},{4,3},{5,4},{6,5},{7,6},{8,7},{9,8},{10,9},{11,1... | collective-permute-start | bytes 786440 | tf_op jit(solution)/shard_map/while/body/eval_jaxpr/ppermute | solution.py:19
  359.7 11.7 %collective-permute-start.2 = (f32[128,512]{1,0:T(8,128)S(1)}, f32[128,512]{1,0:T(8,128)S(1)}, u32[]{:S(2)}, u32[]{:S(2)}) collective-permute-start(f32[128,512]{1,0:T(8,128)S(1)} %get-tuple-element.1333), channel_id=1, source_target_pairs={{1,0},{2,1},{3,2},{4,3},{5,4},{6,5},{7,6},{8,7},{9,8},{10,9},{11,1... | collective-permute-start | bytes 786440 | tf_op jit(solution)/shard_map/while/body/eval_jaxpr/ppermute | solution.py:19
  372.4 12.8 %collective-permute-start.2 = (f32[128,512]{1,0:T(8,128)S(1)}, f32[128,512]{1,0:T(8,128)S(1)}, u32[]{:S(2)}, u32[]{:S(2)}) collective-permute-start(f32[128,512]{1,0:T(8,128)S(1)} %get-tuple-element.1333), channel_id=1, source_target_pairs={{1,0},{2,1},{3,2},{4,3},{5,4},{6,5},{7,6},{8,7},{9,8},{10,9},{11,1... | collective-permute-start | bytes 786440 | tf_op jit(solution)/shard_map/while/body/eval_jaxpr/ppermute | solution.py:19
  (23 other events, 263.3 us)
where the time goes:
time: 567 us; the launch traced here: 564 us
  blocking collectives  175 us (31%)
  waiting for transfers between devices  139 us (25%)
  starting transfers between devices  136 us (24%)
  local copies, waits for them, and re-layouts  47.1 us (8%)
  matrix products  34.2 us (6%)
  other arithmetic  24 us (4%)
  loops' own time  6.87 us (1%)
    psum x1, blocking collectives, local(): grad_bias = lax.psum(jnp.sum(query_grad, axis=0), ('dp', 'ctx'))  175 us
    ppermute x45, waiting for transfers between devices, passed_along(): lax.ppermute(value, axis, [(source, source + steps) for source in range(f...  139 us
    ppermute x45, starting transfers between devices, passed_along(): lax.ppermute(value, axis, [(source, source + steps) for source in range(f...  136 us
    add x15, other arithmetic, return_partial(): returned + lax.dynamic_index_in_dim(partials, window_slots - 1 - step_ind...  14.8 us
  transfers between devices with their start and end apart: 45, of which 30 were waited for; matrix products, arithmetic and copies ran while one was open for 0% of the time, Pallas kernels for 0%

commit v1 on v0

v1 whole, which is shorter than its diff:
```python
import math

import jax
import jax.numpy as jnp
from jax import lax
from jax.experimental import pallas as pl
from jax.experimental.pallas import tpu as pltpu
from jax.sharding import PartitionSpec as P

QUERY_HEADS = 14
GROUPS = 2
PER = 7
D = 128
BLK = 128
NX = 4
NZ = 16
NDP = 8
LEVELS = 4
QW = PER * BLK
LV = NX * BLK
PACK = 2 * BLK + 16
SCALE = 1.0 / math.sqrt(D)
SCALE2 = SCALE * math.log2(math.e)
NEG = -1e30
TILES = ((0, 256), (256, 256), (512, 256), (768, 128))
MESH = pl.DeviceIdType.MESH
F32 = jnp.float32
BF16 = jnp.bfloat16


def dot(a, b):
    return jnp.dot(a, b, preferred_element_type=F32)


def kernel(
    q_ref, k_ref, v_ref, do_ref, doc_ref, bias_ref,
    att_ref, gq_ref, gk_ref, gv_ref, gb_ref,
    kv, pen, qs, qt, dos, dot_t, probs, dsc, mlev, mrow, lrow, ot, dqt, fac,
    own, pout, xret, z2r, csend, crecv, lvl0,
    bdp, bx, bz,
    zs, zr, xs, xr, xs2, xr2, zs2, zr2, cs, cr, bs, br,
):
    ctx = lax.axis_index("ctx")
    dp = lax.axis_index("dp")
    z = ctx // NX
    x = ctx % NX

    def at(dz, dx):
        return {"ctx": ((z + dz + NZ) % NZ) * NX + (x + dx + NX) % NX}

    def at_dp(k):
        return {"dp": (dp + k) % NDP}

    barrier = pltpu.get_barrier_semaphore()
    for k in range(1, NZ):
        pl.semaphore_signal(barrier, inc=1, device_id=at(k, 0), device_id_type=MESH)
    for k in range(1, NX):
        pl.semaphore_signal(barrier, inc=1, device_id=at(0, k), device_id_type=MESH)
    for k in range(1, NDP):
        pl.semaphore_signal(barrier, inc=1, device_id=at_dp(k), device_id_type=MESH)

    def remote(src, dst, send, recv, where):
        return pltpu.make_async_remote_copy(
            src_ref=src, dst_ref=dst, send_sem=send, recv_sem=recv,
            device_id=where, device_id_type=MESH,
        )

    def slot(g, s):
        return kv.at[g, s, pl.ds(0, PACK if g == 0 else 2 * BLK)]

    def z_copy(g, l):
        return remote(slot(g, 4 * l), slot(g, 4 * l + 4), zs.at[g, l], zr.at[g, l], at(1, 0))

    def x_copy(g, l, r):
        return remote(slot(g, 4 * l), slot(g, 4 * l + r), xs.at[g, l, r - 1], xr.at[g, l, r - 1], at(0, r))

    def far_copy(g, r):
        return remote(slot(g, 16), slot(g, r), xs.at[g, 0, r - 1], xr.at[g, 0, r - 1], at(0, r))

    def z2_copy(g, l):
        return remote(slot(g, 4 * l - 2), slot(g, 4 * l + 2), xs.at[g, l, 1], xr.at[g, l, 1], at(1, 0))

    def xret_copy(g, l, r):
        return remote(pout.at[g, 4 * l + r], xret.at[g, l, r - 1], xs2.at[g, l, r - 1], xr2.at[g, l, r - 1], at(0, -r))

    def z2ret_copy(g, l):
        return remote(pout.at[g, 4 * l + 2], z2r.at[g, l - 2], zs2.at[g, l - 2], zr2.at[g, l - 2], at(-1, 0))

    def chain_copy(g, l):
        return remote(csend.at[g, l - 1], crecv.at[g, l - 1], cs.at[g, l - 1], cr.at[g, l - 1], at(-1, 0))

    docs = doc_ref[...].astype(F32)
    for g in range(GROUPS):
        kv[g, 0, 0:BLK, :] = k_ref[:, g * D : (g + 1) * D]
        kv[g, 0, BLK : 2 * BLK, :] = v_ref[:, g * D : (g + 1) * D]
    kv[0, 0, 2 * BLK : PACK, :] = jnp.broadcast_to(docs, (16, BLK)).astype(BF16)

    pl.semaphore_wait(barrier, NZ - 1 + NX - 1 + NDP - 1)

    def start_in(g):
        z_copy(g, 0).start()
        for r in range(1, NX):
            @pl.when(x + r < NX)
            def _(r=r):
                x_copy(g, 0, r).start()

    def service_in(g, l):
        z_copy(g, l - 1).wait_recv()
        if l < 4:
            z_copy(g, l).start()
            for r in (1, 2, 3) if l == 1 else (1, 3):
                x_copy(g, l, r).start()
        else:
            for r in range(1, NX):
                @pl.when(x + r >= NX)
                def _(r=r):
                    far_copy(g, r).start()

    def service_two(g, l):
        x_copy(g, l, 2).wait_recv()
        z2_copy(g, l + 1).start()

    def wait_level(g, l):
        for r in range(1, NX):
            if r == 2 and l in (1, 2):
                continue
            x_copy(g, l, r).wait_recv()

    def prepare():
        for h in range(QUERY_HEADS):
            g, c = h // PER, (h % PER) * BLK
            cols = slice(h * D, (h + 1) * D)
            qh = (q_ref[:, cols].astype(F32) + bias_ref[:, cols]).astype(BF16)
            qs[g, c : c + BLK, :] = qh
            qt[g, :, c : c + BLK] = qh.T
            dh = do_ref[:, cols]
            dos[g, c : c + BLK, :] = dh
            dot_t[g, :, c : c + BLK] = dh.T

    def penalties(l):
        key = lax.broadcasted_iota(jnp.int32, (BLK, BLK), 0).astype(F32)
        for r in range(NX):
            s = 4 * l + r
            kd = kv[0, s, 2 * BLK : PACK, :].astype(F32)[0:1, :]
            zeros = jnp.sum(1.0 - kd, axis=1, keepdims=True)
            limit = docs * zeros
            if l > 0:
                bad = (z < l).astype(F32)
            elif r > 0:
                bad = ((x < r) & (z < 4)).astype(F32)
            else:
                bad = None
            if bad is not None:
                limit = jnp.maximum(limit, bad * float(BLK))
            out = key < limit
            if s == 0:
                out = out | (key > lax.broadcasted_iota(jnp.int32, (BLK, BLK), 1).astype(F32))
            pen[s] = jnp.where(out, NEG, 0.0)

    def level_keys(g, l):
        return kv[g, 4 * l : 4 * l + 4, 0:BLK, :].reshape(LV, D)

    def level_values(g, l):
        return kv[g, 4 * l : 4 * l + 4, BLK : 2 * BLK, :].reshape(LV, D)

    def forward_level(g, l, first):
        keys = level_keys(g, l)
        values_t = level_values(g, l).T
        pn = pen[4 * l : 4 * l + 4].reshape(LV, BLK)
        for c, w in TILES:
            cols = slice(c, c + w)
            s = dot(keys, qt[g, :, cols]) * SCALE2
            s = s + (jnp.concatenate([pn, pn], axis=1) if w == 256 else pn)
            m = jnp.max(s, axis=0, keepdims=True)
            if not first:
                before = mrow[0:1, cols]
                m = jnp.maximum(m, before)
            p = jnp.exp2(s - m)
            total = jnp.sum(p, axis=0, keepdims=True)
            pb = p.astype(BF16)
            probs[l, :, cols] = pb
            o = dot(values_t, pb)
            if not first:
                shrink = jnp.exp2(before - m)
                total = total + lrow[0:1, cols] * shrink
                o = o + ot[:, cols] * shrink
            ot[:, cols] = o
            lrow[0:1, cols] = total
            mrow[0:1, cols] = m
            mlev[l, 0:1, cols] = m

    def normalise(g):
        inverse = 1.0 / lrow[0:1, :]
        for l in range(LEVELS):
            fac[l, 0:1, :] = jnp.exp2(mlev[l, 0:1, :] - mrow[0:1, :]) * inverse
        for j in range(PER):
            cols = slice(j * BLK, (j + 1) * BLK)
            h = g * PER + j
            att_t = ot[:, cols] * inverse[:, cols]
            rounded = att_t.astype(BF16)
            att_ref[:, h * D : (h + 1) * D] = rounded.T
            fac[4, 0:1, cols] = jnp.sum(
                rounded.astype(F32) * dot_t[g, :, cols].astype(F32), axis=0, keepdims=True
            )

    def backward_level(g, l, first):
        keys_t = level_keys(g, l).T
        values = level_values(g, l)
        for c, w in TILES:
            cols = slice(c, c + w)
            dpr = dot(values, dot_t[g, :, cols])
            pn = probs[l, :, cols].astype(F32) * fac[l, 0:1, cols]
            probs[l, :, cols] = pn.astype(BF16)
            ds = (pn * (dpr - fac[4, 0:1, cols])).astype(BF16)
            dsc[:, cols] = ds
            dq = dot(keys_t, ds)
            dqt[:, cols] = dq if first else dqt[:, cols] + dq
        dk = dot(dsc[...], qs[g]) * SCALE
        dv = dot(probs[l], dos[g])
        own[g, l, 0:BLK, :] = dk[0:BLK]
        own[g, l, BLK:, :] = dv[0:BLK]
        for r in range(1, NX):
            rows = slice(r * BLK, (r + 1) * BLK)
            pout[g, 4 * l + r, 0:BLK, :] = dk[rows].astype(BF16)
            pout[g, 4 * l + r, BLK:, :] = dv[rows].astype(BF16)

    def send_back(g, l):
        for r in (1, 2, 3) if l == 0 else (1, 3):
            xret_copy(g, l, r).start()
        if l == 3:
            z2ret_copy(g, 3).start()

    def two_back(g, l):
        z2ret_copy(g, l + 1).wait_recv()
        pout[g, 4 * l + 2] = (pout[g, 4 * l + 2].astype(F32) + z2r[g, l - 1].astype(F32)).astype(BF16)
        if l == 2:
            z2ret_copy(g, 2).start()
        else:
            xret_copy(g, 1, 2).start()

    def chain_first(g):
        near = own[g, 0]
        far = jnp.zeros((2 * BLK, D), F32)
        for r in range(1, NX):
            xret_copy(g, 0, r).wait_recv()
            here = (x + r < NX).astype(F32)
            got = xret[g, 0, r - 1].astype(F32)
            near = near + got * here
            far = far + got * (1.0 - here)
        lvl0[g] = near
        csend[g, 3] = far.astype(BF16)
        chain_copy(g, 4).start()

    def chain_step(g, l):
        total = own[g, l]
        for r in (1, 2, 3) if l == 1 else (1, 3):
            xret_copy(g, l, r).wait_recv()
            total = total + xret[g, l, r - 1].astype(F32)
        chain_copy(g, l + 1).wait_recv()
        csend[g, l - 1] = (total + crecv[g, l].astype(F32)).astype(BF16)
        chain_copy(g, l).start()

    def chain_last(g):
        chain_copy(g, 1).wait_recv()
        total = lvl0[g] + crecv[g, 0].astype(F32)
        gk_ref[:, g * D : (g + 1) * D] = total[0:BLK].astype(BF16)
        gv_ref[:, g * D : (g + 1) * D] = total[BLK:].astype(BF16)

    def finish_queries(g):
        for j in range(PER):
            h = g * PER + j
            dq = (dqt[:, j * BLK : (j + 1) * BLK] * SCALE).T
            gq_ref[:, h * D : (h + 1) * D] = dq.astype(BF16)
            bdp[dp, h : h + 1, :] = jnp.sum(dq, axis=0, keepdims=True)

    def bias_copy(buf, me, k, sem, where):
        return remote(buf.at[me], buf.at[me], bs.at[sem], br.at[sem], where)

    def bias_stage(buf, me, count, base, where):
        for k in range(1, count):
            bias_copy(buf, me, k, base + k, where(k)).start()

    def bias_sum(buf, me, count, base, where):
        for k in range(1, count):
            bias_copy(buf, me, k, base + k, where(k)).wait_recv()
        return jnp.sum(buf[...], axis=0)

    stages = (
        (bdp, dp, NDP, 0, at_dp),
        (bx, x, NX, NDP, lambda k: at(0, k)),
        (bz, z, NZ, NDP + NX, lambda k: at(k, 0)),
    )

    order = (1, 2, 3, 0)
    back = (0, 3, 2, 1)
    start_in(0)
    prepare()
    service_in(0, 1)
    service_in(0, 2)
    service_two(0, 1)
    for i, l in enumerate(order):
        if i == 1:
            service_two(0, 2)
        wait_level(0, l)
        penalties(l)
        forward_level(0, l, i == 0)
        if i == 0:
            service_in(0, 3)
        if i == 1:
            service_in(0, 4)
            start_in(1)
    normalise(0)
    service_in(1, 1)
    backward_level(0, 0, True)
    send_back(0, 0)
    service_in(1, 2)
    service_two(1, 1)
    backward_level(0, 3, False)
    send_back(0, 3)
    service_in(1, 3)
    service_two(1, 2)
    backward_level(0, 2, False)
    send_back(0, 2)
    two_back(0, 2)
    chain_first(0)
    service_in(1, 4)
    backward_level(0, 1, False)
    send_back(0, 1)
    two_back(0, 1)
    finish_queries(0)
    chain_step(0, 3)
    for i, l in enumerate(order):
        wait_level(1, l)
        forward_level(1, l, i == 0)
        if i == 0:
            chain_step(0, 2)
        if i == 1:
            chain_step(0, 1)
        if i == 2:
            chain_last(0)
    normalise(1)
    backward_level(1, 0, True)
    send_back(1, 0)
    backward_level(1, 3, False)
    send_back(1, 3)
    backward_level(1, 2, False)
    send_back(1, 2)
    two_back(1, 2)
    chain_first(1)
    backward_level(1, 1, False)
    send_back(1, 1)
    two_back(1, 1)
    bdp[dp, QUERY_HEADS:16, :] = jnp.zeros((2, D), F32)
    finish_queries(1)
    bias_stage(*stages[0])
    chain_step(1, 3)
    bx[x] = bias_sum(*stages[0])
    bias_stage(*stages[1])
    chain_step(1, 2)
    bz[z] = bias_sum(*stages[1])
    bias_stage(*stages[2])
    chain_step(1, 1)
    chain_last(1)
    gb_ref[...] = bias_sum(*stages[2])

    for g in range(GROUPS):
        for l in range(4):
            z_copy(g, l).wait_send()
            chain_copy(g, l + 1).wait_send()
            for r in range(1, NX):
                x_copy(g, l, r).wait_send()
                if not (r == 2 and l in (2, 3)):
                    xret_copy(g, l, r).wait_send()
        for l in (2, 3):
            z2ret_copy(g, l).wait_send()
    for buf, me, count, base, where in stages:
        for k in range(1, count):
            bias_copy(buf, me, k, base + k, where(k)).wait_send()


def local(query_in, key_in, value_input, output_gradient, doc_ids, query_bias):
    vm = pl.BlockSpec(memory_space=pltpu.VMEM)
    dma = pltpu.SemaphoreType.DMA
    V = pltpu.VMEM
    att, gq, gk, gv, gb = pl.pallas_call(
        kernel,
        out_shape=(
            jax.ShapeDtypeStruct((BLK, QUERY_HEADS * D), BF16),
            jax.ShapeDtypeStruct((BLK, QUERY_HEADS * D), BF16),
            jax.ShapeDtypeStruct((BLK, GROUPS * D), BF16),
            jax.ShapeDtypeStruct((BLK, GROUPS * D), BF16),
            jax.ShapeDtypeStruct((16, D), F32),
        ),
        in_specs=[vm] * 6,
        out_specs=[vm] * 5,
        scratch_shapes=[
            V((GROUPS, 17, PACK, D), BF16),
            V((16, BLK, BLK), F32),
            V((GROUPS, QW, D), BF16),
            V((GROUPS, D, QW), BF16),
            V((GROUPS, QW, D), BF16),
            V((GROUPS, D, QW), BF16),
            V((LEVELS, LV, QW), BF16),
            V((LV, QW), BF16),
            V((LEVELS, 8, QW), F32),
            V((8, QW), F32),
            V((8, QW), F32),
            V((D, QW), F32),
            V((D, QW), F32),
            V((5, 8, QW), F32),
            V((GROUPS, LEVELS, 2 * BLK, D), F32),
            V((GROUPS, 16, 2 * BLK, D), BF16),
            V((GROUPS, LEVELS, 3, 2 * BLK, D), BF16),
            V((GROUPS, 2, 2 * BLK, D), BF16),
            V((GROUPS, 4, 2 * BLK, D), BF16),
            V((GROUPS, 4, 2 * BLK, D), BF16),
            V((GROUPS, 2 * BLK, D), F32),
            V((NDP, 16, D), F32),
            V((NX, 16, D), F32),
            V((NZ, 16, D), F32),
            dma((GROUPS, 4)), dma((GROUPS, 4)),
            dma((GROUPS, 4, 3)), dma((GROUPS, 4, 3)),
            dma((GROUPS, 4, 3)), dma((GROUPS, 4, 3)),
            dma((GROUPS, 2)), dma((GROUPS, 2)),
            dma((GROUPS, 4)), dma((GROUPS, 4)),
            dma((NDP + NX + NZ,)), dma((NDP + NX + NZ,)),
        ],
        compiler_params=pltpu.CompilerParams(
            collective_id=0, has_side_effects=True, vmem_limit_bytes=56 << 20
        ),
    )(
        query_in[0], key_in[0], value_input[0], output_gradient[0], doc_ids, query_bias[None],
    )
    return (att[None], gq[None], gk[None], gv[None], gb[:QUERY_HEADS].reshape(QUERY_HEADS * D))


def solution(mesh):
    rows = P("dp", "ctx", None)
    return jax.shard_map(
        local,
        mesh=mesh,
        in_specs=(rows, rows, rows, rows, P("dp", "ctx"), P()),
        out_specs=(rows, rows, rows, rows, P()),
        check_vma=False,
    )
```

time: 567 us -> 105 us (0.19)
  blocking collectives: 175 us -> 0 us
  waiting for transfers between devices: 139 us -> 0 us
  starting transfers between devices: 136 us -> 0 us
  Pallas kernels: 0 us -> 97.2 us
  local copies, waits for them, and re-layouts: 47.1 us -> 6.81 us
  matrix products: 34.2 us -> 0 us
  other arithmetic: 24 us -> 0 us
  loops' own time: 6.87 us -> 0 us
    psum x1 -> x0, blocking collectives: 175 us -> none  [local(): grad_bias = lax.psum(jnp.sum(query_grad, axis=0), ('dp', 'ctx'))]
    ppermute x45 -> x0, waiting for transfers between devices: 139 us -> none  [passed_along(): lax.ppermute(value, axis, [(source, source + steps) for source in range(f...]
    ppermute x45 -> x0, starting transfers between devices: 136 us -> none  [passed_along(): lax.ppermute(value, axis, [(source, source + steps) for source in range(f...]
    pallas_call x0 -> x1, Pallas kernels: none -> 97.2 us  [local(): pl.pallas_call(kernel, out_shape=(jax.ShapeDtypeStruct((BLK, QUERY_HEADS...]
    dot_general x28 -> x0, matrix products: 34.2 us -> none  [the longest x4 9.28 us: backward_work(): jnp.einsum('qgnd,kgd->gnqk', gradient_heads, value_head_rows, preferred_e...]
    dynamic_update_slice x38 -> x0, local copies, waits for them, and re-layouts: 16 us -> none  [the longest x15 10 us: pass_on(): lax.dynamic_update_index_in_dim(stored_pack, moving_pack, step_index, 0)]
    add x20 -> x0, other arithmetic: 14.8 us -> none  [the longest x15 14.8 us: return_partial(): returned + lax.dynamic_index_in_dim(partials, window_slots - 1 - step_ind...]
    squeeze x9 -> x0, local copies, waits for them, and re-layouts: 9.63 us -> none  [the longest x8 8.66 us: local(): lax.scan(forward_step, start_stats, (window_pack, window_docs, group_ids))]
  transfers between devices with their start and end apart: 45 -> 0, of which waited for: 30 -> 0; matrix products, arithmetic and copies ran while one was open for 0% -> 0% of each run, Pallas kernels for 0% -> 0%
where the time goes in v1:
time: 105 us
  Pallas kernels  97.2 us (93%)
  local copies, waits for them, and re-layouts  6.81 us (6%)
    pallas_call x1, Pallas kernels, local(): pl.pallas_call(kernel, out_shape=(jax.ShapeDtypeStruct((BLK, QUERY_HEADS...  97.2 us
    unnamed x12, local copies, waits for them, and re-layouts  4.92 us

profile of v1, /device:TPU:1, one launch (start us, length us, event | category | flops | bytes accessed | tf_op | source)
XLA Modules:
  0.0 104.6 jit_solution(2400136814732432696)
XLA Ops:
  0.6 1.3 %broadcast_in_dim.15.bias_ref = f32[1,1792]{1,0:T(1,128)} reshape(f32[1792]{0:T(1024)} %param.11) | data formatting | bytes 14336 | tf_op jit(solution)/shard_map/broadcast_in_dim | solution.py:432
  1.9 97.2 %shard_map.101 = (bf16[128,1792]{1,0:T(8,128)(2,1)}, bf16[128,1792]{1,0:T(8,128)(2,1)}, bf16[128,256]{1,0:T(8,128)(2,1)}, bf16[128,256]{1,0:T(8,128)(2,1)}, f32[16,128]{1,0:T(8,128)}) custom-call(bf16[128,1792]{1,0:T(8,128)(2,1)} %bitcast.10, bf16[128,256]{1,0:T(8,128)(2,1)} %bitcast.14, bf16[128,256]{1,0:T(8,128)(2,1)} %bitcast.15, ...), custom_call_target="tpu_custom_call" | custom-call | tf_op jit(solution)/shard_map/pallas_call | solution.py:385
  99.1 0.0 copy-start.3
  99.1 0.7 copy-done.3
  99.8 0.6 slice_bitcast_fusion
  100.4 0.0 copy-start
  100.4 1.9 %copy.15 = bf16[1,128,1792]{2,1,0:T(8,128)(2,1)} copy(bf16[1,128,1792]{2,1,0:T(8,128)(2,1)} %bitcast.13) | data formatting | bytes 917504
  102.3 0.0 copy-done
  102.3 0.0 copy-start.2
  102.3 0.8 copy.16
  103.1 0.1 copy-done.2
  103.2 0.0 copy-start.1
  103.2 0.6 copy.17
  103.8 0.2 copy-done.1
  104.0 0.6 copy.18
Async XLA Ops:
  99.1 0.7 copy-start.3
  100.4 1.9 %copy-start = (bf16[128,1792]{1,0:T(8,128)(2,1)S(1)}, bf16[128,1792]{1,0:T(8,128)(2,1)}, u32[]{:S(2)}) copy-start(bf16[128,1792]{1,0:T(8,128)(2,1)} %get-tuple-element.11) | copy-start | bytes 1376260
  102.3 0.9 copy-start.2
  103.2 0.9 copy-start.1

commit v2 on v1

v2 whole, which is shorter than its diff:
```python
import math

import jax
import jax.numpy as jnp
from jax import lax
from jax.experimental import pallas as pl
from jax.experimental.pallas import tpu as pltpu
from jax.sharding import PartitionSpec as P

QUERY_HEADS = 14
GROUPS = 2
PER = 7
D = 128
BLK = 128
NX = 4
NZ = 16
NDP = 8
LEVELS = 4
QW = PER * BLK
LV = NX * BLK
PACK = 2 * BLK + 16
SCALE = 1.0 / math.sqrt(D)
SCALE2 = SCALE * math.log2(math.e)
NEG = -1e30
TILES = ((0, 256), (256, 256), (512, 256), (768, 128))
MESH = pl.DeviceIdType.MESH
F32 = jnp.float32
BF16 = jnp.bfloat16


def turn(g, l):
    return 1 if l == 2 or (l == 3 and g == 1) else -1


def dot(a, b):
    return jnp.dot(a, b, preferred_element_type=F32)


def kernel(
    q_hbm, k_hbm, v_hbm, do_hbm, doc_ref, bias_ref,
    att_ref, gq_ref, gk_ref, gv_ref, gb_ref,
    q_ref, do_ref, kv, pen, qs, qt, dos, dot_t, probs, dsc, mlev, mrow, lrow, ot, dqt, fac,
    own, pout, xret, csend, crecv, lvl0,
    bdp, bx, bz,
    ins, zs, zr, xs, xr, xs2, xr2, cs, cr, bs, br,
):
    ctx = lax.axis_index("ctx")
    dp = lax.axis_index("dp")
    z = ctx // NX
    x = ctx % NX

    def at(dz, dx):
        return {"ctx": ((z + dz + NZ) % NZ) * NX + (x + dx + NX) % NX}

    def at_dp(k):
        return {"dp": (dp + k) % NDP}

    barrier = pltpu.get_barrier_semaphore()
    for k in range(1, NZ):
        pl.semaphore_signal(barrier, inc=1, device_id=at(k, 0), device_id_type=MESH)
    for k in range(1, NX):
        pl.semaphore_signal(barrier, inc=1, device_id=at(0, k), device_id_type=MESH)
    for k in range(1, NDP):
        pl.semaphore_signal(barrier, inc=1, device_id=at_dp(k), device_id_type=MESH)

    def remote(src, dst, send, recv, where):
        return pltpu.make_async_remote_copy(
            src_ref=src, dst_ref=dst, send_sem=send, recv_sem=recv,
            device_id=where, device_id_type=MESH,
        )

    def slot(g, s):
        return kv.at[g, s, pl.ds(0, PACK if g == 0 else 2 * BLK)]

    def z_copy(g, l):
        source = 4 if l == 3 else 4 * l - 4
        return remote(slot(g, source), slot(g, 4 * l), zs.at[g, l - 1], zr.at[g, l - 1], at(2 if l == 3 else 1, 0))

    def x_copy(g, l, r):
        return remote(slot(g, 4 * l), slot(g, 4 * l + r), xs.at[g, l, r - 1], xr.at[g, l, r - 1], at(0, r))

    def far_copy(g, r):
        return remote(slot(g, 16), slot(g, r), xs.at[g, 0, r - 1], xr.at[g, 0, r - 1], at(0, r))

    def two_copy(g, l):
        d = turn(g, l)
        source = 4 * l + (1 if d > 0 else 3)
        return remote(slot(g, source), slot(g, 4 * l + 2), xs.at[g, l, 1], xr.at[g, l, 1], at(0, d))

    def two_back(g, l):
        return remote(pout.at[g, 4 * l + 2], xret.at[g, l, 1], xs2.at[g, l, 1], xr2.at[g, l, 1], at(0, -turn(g, l)))

    def xret_copy(g, l, r):
        return remote(pout.at[g, 4 * l + r], xret.at[g, l, r - 1], xs2.at[g, l, r - 1], xr2.at[g, l, r - 1], at(0, -r))

    def chain_copy(g, l):
        return remote(csend.at[g, l - 1], crecv.at[g, l - 1], cs.at[g, l - 1], cr.at[g, l - 1], at(-2 if l == 3 else -1, 0))

    def fetch(i, src, dst):
        return pltpu.make_async_copy(src, dst, ins.at[i])

    fetches = [fetch(0, q_hbm, q_ref), fetch(1, do_hbm, do_ref)]
    for g in range(GROUPS):
        lanes = pl.ds(g * D, D)
        fetches.append(fetch(2 + g, k_hbm.at[:, lanes], kv.at[g, 0, pl.ds(0, BLK)]))
        fetches.append(fetch(4 + g, v_hbm.at[:, lanes], kv.at[g, 0, pl.ds(BLK, BLK)]))
    for f in fetches:
        f.start()
    docs = doc_ref[...].astype(F32)
    kv[0, 0, 2 * BLK : PACK, :] = jnp.broadcast_to(docs, (16, BLK)).astype(BF16)
    for f in fetches[2:]:
        f.wait()

    def start_in(g):
        z_copy(g, 1).start()
        for r in range(1, NX):
            @pl.when(x + r < NX)
            def _(r=r):
                x_copy(g, 0, r).start()

    def service_in(g, l):
        z_copy(g, l).wait_recv()
        if l == 1:
            z_copy(g, 2).start()
            z_copy(g, 3).start()
        if l == 3:
            z_copy(g, 4).start()
        if l < 4:
            x_copy(g, l, 1).start()
            x_copy(g, l, 3).start()
        else:
            for r in range(1, NX):
                @pl.when(x + r >= NX)
                def _(r=r):
                    far_copy(g, r).start()

    def service_two(g, l):
        x_copy(g, l, 1 if turn(g, l) > 0 else 3).wait_recv()
        two_copy(g, l).start()

    def wait_level(g, l):
        if l == 0:
            for r in range(1, NX):
                x_copy(g, l, r).wait_recv()
        else:
            x_copy(g, l, 3 if turn(g, l) > 0 else 1).wait_recv()
            two_copy(g, l).wait_recv()

    def prepare():
        for h in range(QUERY_HEADS):
            g, c = h // PER, (h % PER) * BLK
            cols = slice(h * D, (h + 1) * D)
            qh = (q_ref[:, cols].astype(F32) + bias_ref[cols].reshape(1, D)).astype(BF16)
            qs[g, c : c + BLK, :] = qh
            qt[g, :, c : c + BLK] = qh.T
            dh = do_ref[:, cols]
            dos[g, c : c + BLK, :] = dh
            dot_t[g, :, c : c + BLK] = dh.T

    def penalties(l):
        key = lax.broadcasted_iota(jnp.int32, (BLK, BLK), 0).astype(F32)
        for r in range(NX):
            s = 4 * l + r
            kd = kv[0, s, 2 * BLK : PACK, :].astype(F32)[0:1, :]
            zeros = jnp.sum(1.0 - kd, axis=1, keepdims=True)
            limit = docs * zeros
            if l > 0:
                bad = (z < l).astype(F32)
            elif r > 0:
                bad = ((x < r) & (z < 4)).astype(F32)
            else:
                bad = None
            if bad is not None:
                limit = jnp.maximum(limit, bad * float(BLK))
            out = key < limit
            if s == 0:
                out = out | (key > lax.broadcasted_iota(jnp.int32, (BLK, BLK), 1).astype(F32))
            pen[s] = jnp.where(out, NEG, 0.0)

    def level_keys(g, l):
        return kv[g, 4 * l : 4 * l + 4, 0:BLK, :].reshape(LV, D)

    def level_values(g, l):
        return kv[g, 4 * l : 4 * l + 4, BLK : 2 * BLK, :].reshape(LV, D)

    def forward_level(g, l, first):
        keys = level_keys(g, l)
        values_t = level_values(g, l).T
        pn = pen[4 * l : 4 * l + 4].reshape(LV, BLK)
        for c, w in TILES:
            cols = slice(c, c + w)
            s = dot(keys, qt[g, :, cols]) * SCALE2
            s = s + (jnp.concatenate([pn, pn], axis=1) if w == 256 else pn)
            m = jnp.max(s, axis=0, keepdims=True)
            if not first:
                before = mrow[g, 0:1, cols]
                m = jnp.maximum(m, before)
            p = jnp.exp2(s - m)
            total = jnp.sum(p, axis=0, keepdims=True)
            pb = p.astype(BF16)
            probs[g, l, :, cols] = pb
            o = dot(values_t, pb)
            if not first:
                shrink = jnp.exp2(before - m)
                total = total + lrow[g, 0:1, cols] * shrink
                o = o + ot[g, :, cols] * shrink
            ot[g, :, cols] = o
            lrow[g, 0:1, cols] = total
            mrow[g, 0:1, cols] = m
            mlev[g, l, 0:1, cols] = m

    def normalise(g):
        inverse = 1.0 / lrow[g, 0:1, :]
        for l in range(LEVELS):
            fac[g, l, 0:1, :] = jnp.exp2(mlev[g, l, 0:1, :] - mrow[g, 0:1, :]) * inverse
        for j in range(PER):
            cols = slice(j * BLK, (j + 1) * BLK)
            h = g * PER + j
            att_t = ot[g, :, cols] * inverse[:, cols]
            rounded = att_t.astype(BF16)
            att_ref[:, h * D : (h + 1) * D] = rounded.T
            fac[g, 4, 0:1, cols] = jnp.sum(
                rounded.astype(F32) * dot_t[g, :, cols].astype(F32), axis=0, keepdims=True
            )

    def backward_queries(g, l, first):
        keys_t = level_keys(g, l).T
        values = level_values(g, l)
        for c, w in TILES:
            cols = slice(c, c + w)
            dpr = dot(values, dot_t[g, :, cols])
            pn = probs[g, l, :, cols].astype(F32) * fac[g, l, 0:1, cols]
            probs[g, l, :, cols] = pn.astype(BF16)
            ds = (pn * (dpr - fac[g, 4, 0:1, cols])).astype(BF16)
            dsc[g, :, cols] = ds
            dq = dot(keys_t, ds)
            dqt[g, :, cols] = dq if first else dqt[g, :, cols] + dq

    def backward_keys(g, l):
        dk = dot(dsc[g], qs[g]) * SCALE
        dv = dot(probs[g, l], dos[g])
        own[g, l, 0:BLK, :] = dk[0:BLK]
        own[g, l, BLK:, :] = dv[0:BLK]
        for r in range(1, NX):
            rows = slice(r * BLK, (r + 1) * BLK)
            pout[g, 4 * l + r, 0:BLK, :] = dk[rows].astype(BF16)
            pout[g, 4 * l + r, BLK:, :] = dv[rows].astype(BF16)

        if l == 0:
            for r in range(1, NX):
                xret_copy(g, l, r).start()
        else:
            two_back(g, l).start()
            xret_copy(g, l, 3 if turn(g, l) > 0 else 1).start()

    def merge(g, l):
        r = 1 if turn(g, l) > 0 else 3
        two_back(g, l).wait_recv()
        pout[g, 4 * l + r] = (pout[g, 4 * l + r].astype(F32) + xret[g, l, 1].astype(F32)).astype(BF16)
        xret_copy(g, l, r).start()

    def gather(g, l, total):
        for r in (1, 3):
            xret_copy(g, l, r).wait_recv()
            total = total + xret[g, l, r - 1].astype(F32)
        return total

    def chain(g, l):
        if l == 4:
            near = own[g, 0]
            total = jnp.zeros((2 * BLK, D), F32)
            for r in range(1, NX):
                xret_copy(g, 0, r).wait_recv()
                here = (x + r < NX).astype(F32)
                got = xret[g, 0, r - 1].astype(F32)
                near = near + got * here
                total = total + got * (1.0 - here)
            lvl0[g] = near
        else:
            total = gather(g, l, own[g, l])
        for below in {4: (), 3: (4,), 2: (), 1: (2, 3)}[l]:
            chain_copy(g, below).wait_recv()
            total = total + crecv[g, below - 1].astype(F32)
        csend[g, l - 1] = total.astype(BF16)
        chain_copy(g, l).start()

    def chain_last(g):
        chain_copy(g, 1).wait_recv()
        total = lvl0[g] + crecv[g, 0].astype(F32)
        gk_ref[:, g * D : (g + 1) * D] = total[0:BLK].astype(BF16)
        gv_ref[:, g * D : (g + 1) * D] = total[BLK:].astype(BF16)

    def finish_queries(g):
        for j in range(PER):
            h = g * PER + j
            dq = (dqt[g, :, j * BLK : (j + 1) * BLK] * SCALE).T
            gq_ref[:, h * D : (h + 1) * D] = dq.astype(BF16)
            bdp[dp, h : h + 1, :] = jnp.sum(dq, axis=0, keepdims=True)

    def bias_copy(buf, me, k, sem, where):
        return remote(buf.at[me], buf.at[me], bs.at[sem], br.at[sem], where)

    def bias_stage(buf, me, count, base, where):
        for k in range(1, count):
            bias_copy(buf, me, k, base + k, where(k)).start()

    def bias_sum(buf, me, count, base, where):
        for k in range(1, count):
            bias_copy(buf, me, k, base + k, where(k)).wait_recv()
        return jnp.sum(buf[...], axis=0)

    stages = (
        (bdp, dp, NDP, 0, at_dp),
        (bx, x, NX, NDP, lambda k: at(0, k)),
        (bz, z, NZ, NDP + NX, lambda k: at(k, 0)),
    )

    def forward(g, l, first=False):
        wait_level(g, l)
        if g == 0:
            penalties(l)
        forward_level(g, l, first)

    def backward(g, l, first=False):
        backward_queries(g, l, first)
        backward_keys(g, l)

    pl.semaphore_wait(barrier, NZ - 1 + NX - 1 + NDP - 1)
    start_in(0)
    start_in(1)
    for f in fetches[:2]:
        f.wait()
    prepare()
    service_in(0, 1)
    service_in(1, 1)
    service_two(0, 1)
    service_in(0, 2)
    service_in(0, 3)
    service_two(1, 1)
    service_in(1, 2)
    service_in(1, 3)
    forward(0, 1, True)
    service_in(0, 4)
    service_two(0, 2)
    service_two(0, 3)
    forward(1, 1, True)
    service_in(1, 4)
    service_two(1, 2)
    service_two(1, 3)
    forward(0, 2)
    forward(0, 3)
    forward(0, 0)
    normalise(0)
    backward(0, 0, True)
    forward(1, 2)
    backward(0, 3)
    forward(1, 3)
    chain(0, 4)
    forward(1, 0)
    normalise(1)
    merge(0, 3)
    backward(1, 0, True)
    backward(0, 2)
    chain(0, 3)
    backward(1, 3)
    merge(0, 2)
    chain(1, 4)
    backward(0, 1)
    merge(1, 3)
    finish_queries(0)
    backward(1, 2)
    chain(0, 2)
    merge(0, 1)
    backward_queries(1, 1, False)
    bdp[dp, QUERY_HEADS:16, :] = jnp.zeros((2, D), F32)
    finish_queries(1)
    bias_stage(*stages[0])
    backward_keys(1, 1)
    merge(1, 2)
    chain(1, 3)
    bx[x] = bias_sum(*stages[0])
    bias_stage(*stages[1])
    merge(1, 1)
    chain(0, 1)
    chain(1, 2)
    bz[z] = bias_sum(*stages[1])
    bias_stage(*stages[2])
    chain(1, 1)
    chain_last(0)
    chain_last(1)
    gb_ref[...] = bias_sum(*stages[2])

    for g in range(GROUPS):
        for l in range(4):
            z_copy(g, l + 1).wait_send()
            chain_copy(g, l + 1).wait_send()
            for r in range(1, NX):
                if r == 2 and l > 0:
                    two_copy(g, l).wait_send()
                    two_back(g, l).wait_send()
                else:
                    x_copy(g, l, r).wait_send()
                    xret_copy(g, l, r).wait_send()
    for buf, me, count, base, where in stages:
        for k in range(1, count):
            bias_copy(buf, me, k, base + k, where(k)).wait_send()


def hand_over(att, gq, gk, gv, gb, att_out, gq_out, gk_out, gv_out, gb_out, sem):
    pairs = ((att, att_out), (gq, gq_out), (gk, gk_out), (gv, gv_out))
    copies = [pltpu.make_async_copy(a, b.at[0], sem.at[i]) for i, (a, b) in enumerate(pairs)]
    for c in copies:
        c.start()
    for h in range(QUERY_HEADS):
        gb_out[h * D : (h + 1) * D] = gb[h, :]
    for c in copies:
        c.wait()


def local(query_in, key_in, value_input, output_gradient, doc_ids, query_bias):
    vm = pl.BlockSpec(memory_space=pltpu.VMEM)
    anyspace = pl.BlockSpec(memory_space=pl.ANY)
    dma = pltpu.SemaphoreType.DMA
    V = pltpu.VMEM
    att, gq, gk, gv, gb = pl.pallas_call(
        kernel,
        out_shape=(
            jax.ShapeDtypeStruct((BLK, QUERY_HEADS * D), BF16),
            jax.ShapeDtypeStruct((BLK, QUERY_HEADS * D), BF16),
            jax.ShapeDtypeStruct((BLK, GROUPS * D), BF16),
            jax.ShapeDtypeStruct((BLK, GROUPS * D), BF16),
            jax.ShapeDtypeStruct((16, D), F32),
        ),
        in_specs=[anyspace] * 4 + [vm] * 2,
        out_specs=[vm] * 5,
        scratch_shapes=[
            V((BLK, QUERY_HEADS * D), BF16),
            V((BLK, QUERY_HEADS * D), BF16),
            V((GROUPS, 17, PACK, D), BF16),
            V((16, BLK, BLK), F32),
            V((GROUPS, QW, D), BF16),
            V((GROUPS, D, QW), BF16),
            V((GROUPS, QW, D), BF16),
            V((GROUPS, D, QW), BF16),
            V((GROUPS, LEVELS, LV, QW), BF16),
            V((GROUPS, LV, QW), BF16),
            V((GROUPS, LEVELS, 8, QW), F32),
            V((GROUPS, 8, QW), F32),
            V((GROUPS, 8, QW), F32),
            V((GROUPS, D, QW), F32),
            V((GROUPS, D, QW), F32),
            V((GROUPS, 5, 8, QW), F32),
            V((GROUPS, LEVELS, 2 * BLK, D), F32),
            V((GROUPS, 16, 2 * BLK, D), BF16),
            V((GROUPS, LEVELS, 3, 2 * BLK, D), BF16),
            V((GROUPS, 4, 2 * BLK, D), BF16),
            V((GROUPS, 4, 2 * BLK, D), BF16),
            V((GROUPS, 2 * BLK, D), F32),
            V((NDP, 16, D), F32),
            V((NX, 16, D), F32),
            V((NZ, 16, D), F32),
            dma((6,)),
            dma((GROUPS, 4)), dma((GROUPS, 4)),
            dma((GROUPS, 4, 3)), dma((GROUPS, 4, 3)),
            dma((GROUPS, 4, 3)), dma((GROUPS, 4, 3)),
            dma((GROUPS, 4)), dma((GROUPS, 4)),
            dma((NDP + NX + NZ,)), dma((NDP + NX + NZ,)),
        ],
        compiler_params=pltpu.CompilerParams(
            collective_id=0, has_side_effects=True, vmem_limit_bytes=56 << 20
        ),
    )(
        query_in[0], key_in[0], value_input[0], output_gradient[0], doc_ids, query_bias,
    )
    return pl.pallas_call(
        hand_over,
        out_shape=(
            jax.ShapeDtypeStruct((1, BLK, QUERY_HEADS * D), BF16),
            jax.ShapeDtypeStruct((1, BLK, QUERY_HEADS * D), BF16),
            jax.ShapeDtypeStruct((1, BLK, GROUPS * D), BF16),
            jax.ShapeDtypeStruct((1, BLK, GROUPS * D), BF16),
            jax.ShapeDtypeStruct((QUERY_HEADS * D,), F32),
        ),
        in_specs=[vm] * 5,
        out_specs=[anyspace] * 4 + [vm],
        scratch_shapes=[dma((4,))],
    )(att, gq, gk, gv, gb)


def solution(mesh):
    rows = P("dp", "ctx", None)
    return jax.shard_map(
        local,
        mesh=mesh,
        in_specs=(rows, rows, rows, rows, P("dp", "ctx"), P()),
        out_specs=(rows, rows, rows, rows, P()),
        check_vma=False,
    )
```

time: 105 us -> 93.7 us (0.89)
  local copies, waits for them, and re-layouts: 6.81 us -> 0 us
  Pallas kernels: 97.2 us -> 92.7 us
    pallas_call x1, Pallas kernels: 97.2 us -> 89.9 us  [local(): pl.pallas_call(kernel, out_shape=(jax.ShapeDtypeStruct((BLK, QUERY_HEADS...]
    unnamed x12 -> x0, local copies, waits for them, and re-layouts: 4.92 us -> none
    pallas_call x0 -> x1, Pallas kernels: none -> 2.77 us  [local(): pl.pallas_call(hand_over, out_shape=(jax.ShapeDtypeStruct((1, BLK, QUERY_...]
    broadcast_in_dim x1 -> x0, local copies, waits for them, and re-layouts: 1.3 us -> none  [local(): query_bias[None]]
where the time goes in v2:
time: 93.7 us; the launch traced here: 93.5 us
  Pallas kernels  92.7 us (99%)
    pallas_call x1, Pallas kernels, local(): pl.pallas_call(kernel, out_shape=(jax.ShapeDtypeStruct((BLK, QUERY_HEADS...  89.9 us
    pallas_call x1, Pallas kernels, local(): pl.pallas_call(hand_over, out_shape=(jax.ShapeDtypeStruct((1, BLK, QUERY_...  2.77 us

profile of v2, /device:TPU:1, one launch (start us, length us, event | category | flops | bytes accessed | tf_op | source)
XLA Modules:
  0.0 93.5 jit_solution(9993006338055451464)
XLA Ops:
  0.6 89.9 %shard_map.101 = (bf16[128,1792]{1,0:T(8,128)(2,1)}, bf16[128,1792]{1,0:T(8,128)(2,1)}, bf16[128,256]{1,0:T(8,128)(2,1)}, bf16[128,256]{1,0:T(8,128)(2,1)}, f32[16,128]{1,0:T(8,128)}) custom-call(bf16[128,1792]{1,0:T(8,128)(2,1)} %bitcast.4, bf16[128,256]{1,0:T(8,128)(2,1)} %bitcast.6, bf16[128,256]{1,0:T(8,128)(2,1)} %bitcast.7, bf16[128,1792]{1,0:T(8,128)(2,1)} %bitcast.5, ...), custom_call_target="tpu_custom_call" | custom-call | tf_op jit(solution)/shard_map/pallas_call | solution.py:425
  90.6 2.8 %shard_map.102 = (bf16[1,128,1792]{2,1,0:T(8,128)(2,1)}, bf16[1,128,1792]{2,1,0:T(8,128)(2,1)}, bf16[1,128,256]{2,1,0:T(8,128)(2,1)}, bf16[1,128,256]{2,1,0:T(8,128)(2,1)}, f32[1792]{0:T(1024)}) custom-call(bf16[128,1792]{1,0:T(8,128)(2,1)} %get-tuple-element.10.att, bf16[128,1792]{1,0:T(8,128)(2,1)} %get-tuple-element.11.gq, ...), custom_call_target="tpu_custom_call" | custom-call | tf_op jit(solution)/shard_map/pallas_call | solution.py:475

commit v3 on v2

--- a/solution.py
+++ b/solution.py
@@ -32,6 +32,10 @@
     return 1 if l == 2 or (l == 3 and g == 1) else -1
 
 
+def straight(g, l):
+    return g == 0 and l in (1, 2)
+
+
 def dot(a, b):
     return jnp.dot(a, b, preferred_element_type=F32)
 
@@ -56,12 +60,17 @@
         return {"dp": (dp + k) % NDP}
 
     barrier = pltpu.get_barrier_semaphore()
-    for k in range(1, NZ):
-        pl.semaphore_signal(barrier, inc=1, device_id=at(k, 0), device_id_type=MESH)
+    def greet(where):
+        pl.semaphore_signal(barrier, inc=1, device_id=where, device_id_type=MESH)
+
+    for k in (-1, 1, -2, 2):
+        greet(at(k, 0))
     for k in range(1, NX):
-        pl.semaphore_signal(barrier, inc=1, device_id=at(0, k), device_id_type=MESH)
+        greet(at(0, k))
     for k in range(1, NDP):
-        pl.semaphore_signal(barrier, inc=1, device_id=at_dp(k), device_id_type=MESH)
+        greet(at_dp(k))
+    for k in range(3, NZ - 2):
+        greet(at(k, 0))
 
     def remote(src, dst, send, recv, where):
         return pltpu.make_async_remote_copy(
@@ -111,35 +120,42 @@
     for f in fetches[2:]:
         f.wait()
 
-    def start_in(g):
-        z_copy(g, 1).start()
+    def near_in(g):
         for r in range(1, NX):
             @pl.when(x + r < NX)
             def _(r=r):
                 x_copy(g, 0, r).start()
 
-    def service_in(g, l):
-        z_copy(g, l).wait_recv()
+    def along_z(g, l):
         if l == 1:
+            z_copy(g, 3).start()
             z_copy(g, 2).start()
-            z_copy(g, 3).start()
         if l == 3:
             z_copy(g, 4).start()
+
+    def along_x(g, l):
         if l < 4:
             x_copy(g, l, 1).start()
             x_copy(g, l, 3).start()
+            if straight(g, l):
+                x_copy(g, l, 2).start()
         else:
             for r in range(1, NX):
                 @pl.when(x + r >= NX)
                 def _(r=r):
                     far_copy(g, r).start()
 
+    def service_in(g, l):
+        z_copy(g, l).wait_recv()
+        along_z(g, l)
+        along_x(g, l)
+
     def service_two(g, l):
         x_copy(g, l, 1 if turn(g, l) > 0 else 3).wait_recv()
         two_copy(g, l).start()
 
     def wait_level(g, l):
-        if l == 0:
+        if l == 0 or straight(g, l):
             for r in range(1, NX):
                 x_copy(g, l, r).wait_recv()
         else:
@@ -232,12 +248,12 @@
             pn = probs[g, l, :, cols].astype(F32) * fac[g, l, 0:1, cols]
             probs[g, l, :, cols] = pn.astype(BF16)
             ds = (pn * (dpr - fac[g, 4, 0:1, cols])).astype(BF16)
-            dsc[g, :, cols] = ds
+            dsc[g, l, :, cols] = ds
             dq = dot(keys_t, ds)
             dqt[g, :, cols] = dq if first else dqt[g, :, cols] + dq
 
     def backward_keys(g, l):
-        dk = dot(dsc[g], qs[g]) * SCALE
+        dk = dot(dsc[g, l], qs[g]) * SCALE
         dv = dot(probs[g, l], dos[g])
         own[g, l, 0:BLK, :] = dk[0:BLK]
         own[g, l, BLK:, :] = dv[0:BLK]
@@ -246,7 +262,7 @@
             pout[g, 4 * l + r, 0:BLK, :] = dk[rows].astype(BF16)
             pout[g, 4 * l + r, BLK:, :] = dv[rows].astype(BF16)
 
-        if l == 0:
+        if l < 3:
             for r in range(1, NX):
                 xret_copy(g, l, r).start()
         else:
@@ -260,7 +276,7 @@
         xret_copy(g, l, r).start()
 
     def gather(g, l, total):
-        for r in (1, 3):
+        for r in (1, 3) if l == 3 else (1, 2, 3):
             xret_copy(g, l, r).wait_recv()
             total = total + xret[g, l, r - 1].astype(F32)
         return total
@@ -295,7 +311,15 @@
             h = g * PER + j
             dq = (dqt[g, :, j * BLK : (j + 1) * BLK] * SCALE).T
             gq_ref[:, h * D : (h + 1) * D] = dq.astype(BF16)
-            bdp[dp, h : h + 1, :] = jnp.sum(dq, axis=0, keepdims=True)
+
+    def bias_rows():
+        lane = lax.broadcasted_iota(jnp.int32, (D, BLK), 1)
+        columns = jnp.zeros((D, BLK), F32)
+        for h in range(QUERY_HEADS):
+            c = (h % PER) * BLK
+            total = jnp.sum(dqt[h // PER, :, c : c + BLK], axis=1, keepdims=True) * SCALE
+            columns = jnp.where(lane == h, total, columns)
+        bdp[dp] = columns.T[0:16]
 
     def bias_copy(buf, me, k, sem, where):
         return remote(buf.at[me], buf.at[me], bs.at[sem], br.at[sem], where)
@@ -326,29 +350,31 @@
         backward_keys(g, l)
 
     pl.semaphore_wait(barrier, NZ - 1 + NX - 1 + NDP - 1)
-    start_in(0)
-    start_in(1)
+    z_copy(0, 1).start()
+    z_copy(1, 1).start()
+    near_in(0)
     for f in fetches[:2]:
         f.wait()
     prepare()
     service_in(0, 1)
-    service_in(1, 1)
-    service_two(0, 1)
+    z_copy(1, 1).wait_recv()
+    along_x(1, 1)
+    near_in(1)
+    service_in(0, 3)
     service_in(0, 2)
-    service_in(0, 3)
+    along_z(1, 1)
     service_two(1, 1)
+    forward(0, 1, True)
+    service_two(0, 3)
+    service_in(0, 4)
+    forward(1, 1, True)
+    service_in(1, 3)
     service_in(1, 2)
-    service_in(1, 3)
-    forward(0, 1, True)
-    service_in(0, 4)
-    service_two(0, 2)
-    service_two(0, 3)
-    forward(1, 1, True)
-    service_in(1, 4)
-    service_two(1, 2)
-    service_two(1, 3)
     forward(0, 2)
     forward(0, 3)
+    service_two(1, 3)
+    service_two(1, 2)
+    service_in(1, 4)
     forward(0, 0)
     normalise(0)
     backward(0, 0, True)
@@ -358,33 +384,32 @@
     chain(0, 4)
     forward(1, 0)
     normalise(1)
+    backward(1, 0, True)
     merge(0, 3)
-    backward(1, 0, True)
-    backward(0, 2)
+    backward(1, 3)
+    backward_queries(0, 2, False)
+    backward_queries(0, 1, False)
+    chain(1, 4)
+    backward_queries(1, 2, False)
+    backward_queries(1, 1, False)
+    bias_rows()
+    bias_stage(*stages[0])
+    backward_keys(0, 2)
     chain(0, 3)
-    backward(1, 3)
-    merge(0, 2)
-    chain(1, 4)
-    backward(0, 1)
     merge(1, 3)
-    finish_queries(0)
-    backward(1, 2)
-    chain(0, 2)
-    merge(0, 1)
-    backward_queries(1, 1, False)
-    bdp[dp, QUERY_HEADS:16, :] = jnp.zeros((2, D), F32)
-    finish_queries(1)
-    bias_stage(*stages[0])
+    backward_keys(1, 2)
+    backward_keys(0, 1)
     backward_keys(1, 1)
-    merge(1, 2)
-    chain(1, 3)
     bx[x] = bias_sum(*stages[0])
     bias_stage(*stages[1])
-    merge(1, 1)
-    chain(0, 1)
+    chain(1, 3)
+    chain(0, 2)
     chain(1, 2)
+    finish_queries(0)
     bz[z] = bias_sum(*stages[1])
     bias_stage(*stages[2])
+    finish_queries(1)
+    chain(0, 1)
     chain(1, 1)
     chain_last(0)
     chain_last(1)
@@ -395,11 +420,13 @@
             z_copy(g, l + 1).wait_send()
             chain_copy(g, l + 1).wait_send()
             for r in range(1, NX):
-                if r == 2 and l > 0:
+                if r == 2 and l > 0 and not straight(g, l):
                     two_copy(g, l).wait_send()
+                else:
+                    x_copy(g, l, r).wait_send()
+                if r == 2 and l == 3:
                     two_back(g, l).wait_send()
                 else:
-                    x_copy(g, l, r).wait_send()
                     xret_copy(g, l, r).wait_send()
     for buf, me, count, base, where in stages:
         for k in range(1, count):
@@ -443,7 +470,7 @@
             V((GROUPS, QW, D), BF16),
             V((GROUPS, D, QW), BF16),
             V((GROUPS, LEVELS, LV, QW), BF16),
-            V((GROUPS, LV, QW), BF16),
+            V((GROUPS, LEVELS, LV, QW), BF16),
             V((GROUPS, LEVELS, 8, QW), F32),
             V((GROUPS, 8, QW), F32),
             V((GROUPS, 8, QW), F32),

time: 93.7 us -> 89.8 us (0.958)
  the two profiles are of different devices: /device:TPU:1 before, /device:TPU:8 now
where the time goes in v3:
time: 89.8 us; the launch traced here: 89.6 us
  Pallas kernels  88.8 us (99%)
    pallas_call x1, Pallas kernels, local(): pl.pallas_call(kernel, out_shape=(jax.ShapeDtypeStruct((BLK, QUERY_HEADS...  86.1 us
    pallas_call x1, Pallas kernels, local(): pl.pallas_call(hand_over, out_shape=(jax.ShapeDtypeStruct((1, BLK, QUERY_...  2.77 us

profile of v3, /device:TPU:8, one launch (start us, length us, event | category | flops | bytes accessed | tf_op | source)
XLA Modules:
  0.0 89.6 jit_solution(13234980889478097969)
XLA Ops:
  0.6 86.1 %shard_map.101 = (bf16[128,1792]{1,0:T(8,128)(2,1)}, bf16[128,1792]{1,0:T(8,128)(2,1)}, bf16[128,256]{1,0:T(8,128)(2,1)}, bf16[128,256]{1,0:T(8,128)(2,1)}, f32[16,128]{1,0:T(8,128)}) custom-call(bf16[128,1792]{1,0:T(8,128)(2,1)} %bitcast.4, bf16[128,256]{1,0:T(8,128)(2,1)} %bitcast.6, bf16[128,256]{1,0:T(8,128)(2,1)} %bitcast.7, bf16[128,1792]{1,0:T(8,128)(2,1)} %bitcast.5, ...), custom_call_target="tpu_custom_call" | custom-call | tf_op jit(solution)/shard_map/pallas_call | solution.py:452
  86.7 2.8 %shard_map.102 = (bf16[1,128,1792]{2,1,0:T(8,128)(2,1)}, bf16[1,128,1792]{2,1,0:T(8,128)(2,1)}, bf16[1,128,256]{2,1,0:T(8,128)(2,1)}, bf16[1,128,256]{2,1,0:T(8,128)(2,1)}, f32[1792]{0:T(1024)}) custom-call(bf16[128,1792]{1,0:T(8,128)(2,1)} %get-tuple-element.10.att, bf16[128,1792]{1,0:T(8,128)(2,1)} %get-tuple-element.11.gq, ...), custom_call_target="tpu_custom_call" | custom-call | tf_op jit(solution)/shard_map/pallas_call | solution.py:502

commit v4 on v3

--- a/solution.py
+++ b/solution.py
@@ -400,10 +400,10 @@
     backward_keys(1, 2)
     backward_keys(0, 1)
     backward_keys(1, 1)
+    chain(1, 3)
+    chain(0, 2)
     bx[x] = bias_sum(*stages[0])
     bias_stage(*stages[1])
-    chain(1, 3)
-    chain(0, 2)
     chain(1, 2)
     finish_queries(0)
     bz[z] = bias_sum(*stages[1])

time: 89.8 us -> 89.8 us (level)
  no operation moved by 1% of the time
where the time goes in v4:
time: 89.8 us; the launch traced here: 89.6 us
  Pallas kernels  88.8 us (99%)
    pallas_call x1, Pallas kernels, local(): pl.pallas_call(kernel, out_shape=(jax.ShapeDtypeStruct((BLK, QUERY_HEADS...  86.1 us
    pallas_call x1, Pallas kernels, local(): pl.pallas_call(hand_over, out_shape=(jax.ShapeDtypeStruct((1, BLK, QUERY_...  2.77 us

profile of v4, /device:TPU:8, one launch (start us, length us, event | category | flops | bytes accessed | tf_op | source)
XLA Modules:
  0.0 89.6 jit_solution(10713030618769616153)
XLA Ops:
  0.6 86.1 %shard_map.101 = (bf16[128,1792]{1,0:T(8,128)(2,1)}, bf16[128,1792]{1,0:T(8,128)(2,1)}, bf16[128,256]{1,0:T(8,128)(2,1)}, bf16[128,256]{1,0:T(8,128)(2,1)}, f32[16,128]{1,0:T(8,128)}) custom-call(bf16[128,1792]{1,0:T(8,128)(2,1)} %bitcast.4, bf16[128,256]{1,0:T(8,128)(2,1)} %bitcast.6, bf16[128,256]{1,0:T(8,128)(2,1)} %bitcast.7, bf16[128,1792]{1,0:T(8,128)(2,1)} %bitcast.5, ...), custom_call_target="tpu_custom_call" | custom-call | tf_op jit(solution)/shard_map/pallas_call | solution.py:452
  86.7 2.8 %shard_map.102 = (bf16[1,128,1792]{2,1,0:T(8,128)(2,1)}, bf16[1,128,1792]{2,1,0:T(8,128)(2,1)}, bf16[1,128,256]{2,1,0:T(8,128)(2,1)}, bf16[1,128,256]{2,1,0:T(8,128)(2,1)}, f32[1792]{0:T(1024)}) custom-call(bf16[128,1792]{1,0:T(8,128)(2,1)} %get-tuple-element.10.att, bf16[128,1792]{1,0:T(8,128)(2,1)} %get-tuple-element.11.gq, ...), custom_call_target="tpu_custom_call" | custom-call | tf_op jit(solution)/shard_map/pallas_call | solution.py:502
